TPU v7x, 32 devices: a whole 2x2x4 slice. The times are simulated.
32 devices in a mesh: hid: 8 (over y, x, core), tok: 4 (over z).
Axes of the slice: x: 2, y: 2, z: 4, core: 2. Of those that a mesh axis runs over, the one named last changes fastest.
Arguments:
- tokens: bfloat16 [896, 8192], P('tok', 'hid'), may hold values from -6 to 6
- in_blocks: bfloat16 [128, 6, 256, 256], P('hid', None, 'tok'), may hold values from -0.15625 to 0.15625
- in_left: bfloat16 [8192, 256], P(('hid', 'tok')), may hold values from -0.0625 to 0.0625
- in_right: bfloat16 [256, 32768], P(None, ('hid', 'tok')), may hold values from -0.375 to 0.375
- in_lists: int32 [128, 6], replicated, may hold values from 0 to 31, as said below
- out_blocks: bfloat16 [128, 6, 256, 256], P('hid', None, 'tok'), may hold values from -0.078125 to 0.078125
- out_left: bfloat16 [32768, 256], P(('hid', 'tok')), may hold values from -0.03125 to 0.03125
- out_right: bfloat16 [256, 8192], P(None, ('hid', 'tok')), may hold values from -0.375 to 0.375
- out_lists: int32 [128, 6], replicated, may hold values from 0 to 31, as said below
- cotangent: bfloat16 [896, 8192], P('tok', 'hid'), may hold values from -6 to 6
Outputs:
- layer_out: bfloat16 [896, 8192], P('tok', 'hid')
- grad_tokens: bfloat16 [896, 8192], P('tok', 'hid')
- grad_in_blocks: bfloat16 [128, 6, 256, 256], P('hid', None, 'tok')
- grad_in_left: bfloat16 [8192, 256], P(('hid', 'tok'))
- grad_in_right: bfloat16 [256, 32768], P(None, ('hid', 'tok'))
- grad_out_blocks: bfloat16 [128, 6, 256, 256], P('hid', None, 'tok')
- grad_out_left: bfloat16 [32768, 256], P(('hid', 'tok'))
- grad_out_right: bfloat16 [256, 8192], P(None, ('hid', 'tok'))
Inputs may be any that keep to these rules, and one draw needn't show every extreme that they name: There is one whole number m, the same for every row, with in_lists[c, 0] = ((c * 8192) // 32768) XOR m, and in_lists[c, k] = in_lists[c, 0] XOR 2^(k-1) for k = 1 to 5. `out_lists`: the same butterfly form as in_lists, with its own number m, which differs from that of in_lists.
All inputs are finite; a program needn't handle non-finite values.
Results may differ from a plain program's by a relative error of at most 0.012.
Values may be sent and summed in bfloat16 or wider, within the bound.
A program may use at most 256 MiB of HBM per device.

v0:
```python
import jax
import jax.numpy as jnp
from jax import lax
from jax.sharding import PartitionSpec as P

D = 8192
BLK = 256


def gelu_parts(preact):
    inner_coef = 0.7978845608028654
    cubic_coef = 0.044715
    inner_arg = inner_coef * (preact + cubic_coef * preact * preact * preact)
    tanh_val = jnp.tanh(inner_arg)
    active = 0.5 * preact * (1.0 + tanh_val)
    slopes = 0.5 * (1.0 + tanh_val) + 0.5 * preact * (1.0 - tanh_val * tanh_val) * inner_coef * (
        1.0 + 3.0 * cubic_coef * preact * preact
    )
    return (active, slopes)


def dot_rows(left_arr, right_arr):
    return lax.dot_general(
        left_arr, right_arr, (((0,), (0,)), ((), ())), preferred_element_type=jnp.float32
    )


def dot_cols(left_arr, right_arr):
    return lax.dot_general(
        left_arr, right_arr, (((1,), (1,)), ((), ())), preferred_element_type=jnp.float32
    )


def rank_sum(values):
    return lax.psum(values, "hid")


def own_lists(lists, hid_blocks):
    return lax.dynamic_slice_in_dim(lists, lax.axis_index("hid") * hid_blocks, hid_blocks, 0)


def gather_in(values, lists, hid_blocks, blk_width):
    whole = lax.all_gather(values, "hid", axis=1, tiled=True)
    mine = own_lists(lists, hid_blocks)
    blocks = whole.reshape(whole.shape[0], whole.shape[1] // blk_width, blk_width)
    return blocks[:, mine.T]


def scatter_out(parts, lists, hid_blocks):
    mine = own_lists(lists, hid_blocks)
    picker = (mine.T[:, :, None] == jnp.arange(D // BLK, dtype=jnp.int32)[None, None, :]).astype(
        jnp.float32
    )
    dense = jnp.einsum("nsho,shc->nco", parts, picker, precision=lax.Precision.HIGHEST)
    return lax.psum_scatter(
        dense.reshape(dense.shape[0], -1), "hid", scatter_dimension=1, tiled=True
    )


def route_in(values, lists, hid_blocks, blk_width):
    return gather_in(values, lists, hid_blocks, blk_width)


def route_out(parts, lists, hid_blocks):
    return scatter_out(parts, lists, hid_blocks)


def local(
    tokens,
    in_blocks,
    in_left,
    in_right,
    in_lists,
    out_blocks,
    out_left,
    out_right,
    out_lists,
    cotangent,
):
    row_count, col_span = tokens.shape
    hid_blocks = in_blocks.shape[0]
    slot_count = in_blocks.shape[1]
    blk_width = in_blocks.shape[3]
    tok_count = lax.axis_size("tok")
    w_first, w_second, left_one, right_one, left_two, right_two = (
        lax.all_gather(in_blocks, "tok", axis=2, tiled=True),
        lax.all_gather(out_blocks, "tok", axis=2, tiled=True),
        lax.all_gather(in_left, "tok", axis=0, tiled=True),
        lax.all_gather(in_right, "tok", axis=1, tiled=True),
        lax.all_gather(out_left, "tok", axis=0, tiled=True),
        lax.all_gather(out_right, "tok", axis=1, tiled=True),
    )
    low_in, low_back = rank_sum(
        (
            jnp.dot(tokens, left_one, preferred_element_type=jnp.float32),
            dot_cols(cotangent, right_two),
        )
    )
    low_in = low_in.astype(jnp.bfloat16)
    low_back = low_back.astype(jnp.bfloat16)
    gathered = route_in(tokens, in_lists, hid_blocks, blk_width)
    group_count = gathered.shape[2]
    per_group = hid_blocks // group_count
    first_r = w_first.reshape(group_count, per_group, slot_count, blk_width, blk_width)
    second_r = w_second.reshape(group_count, per_group, slot_count, blk_width, blk_width)
    preact = jnp.einsum(
        "nseb,eqsbf->neqf", gathered, first_r, preferred_element_type=jnp.float32
    ).reshape(row_count, -1)
    preact = preact + jnp.dot(low_in, right_one, preferred_element_type=jnp.float32)
    active, slopes = gelu_parts(preact)
    hidden = active.astype(jnp.bfloat16)
    low_mid = rank_sum(jnp.dot(hidden, left_two, preferred_element_type=jnp.float32)).astype(
        jnp.bfloat16
    )
    hidden_r = hidden.reshape(row_count, group_count, per_group, blk_width)
    out_parts = jnp.einsum(
        "neqf,eqsfo->nseo", hidden_r, second_r, preferred_element_type=jnp.float32
    )
    sparse_out = route_out(out_parts, out_lists, hid_blocks)
    layer_out = (
        sparse_out + jnp.dot(low_mid, right_two, preferred_element_type=jnp.float32)
    ).astype(jnp.bfloat16)
    grad_in = route_in(cotangent, out_lists, hid_blocks, blk_width)
    grad_hidden = jnp.einsum(
        "nseo,eqsfo->neqf", grad_in, second_r, preferred_element_type=jnp.float32
    ).reshape(row_count, -1)
    grad_hidden = grad_hidden + dot_cols(low_back, left_two)
    grad_pre = (grad_hidden * slopes).astype(jnp.bfloat16)
    low_grad = rank_sum(dot_cols(grad_pre, right_one)).astype(jnp.bfloat16)
    grad_pre_r = grad_pre.reshape(row_count, group_count, per_group, blk_width)
    back_parts = jnp.einsum(
        "neqf,eqsbf->nseb", grad_pre_r, first_r, preferred_element_type=jnp.float32
    )
    sparse_back = route_out(back_parts, in_lists, hid_blocks)
    grad_tokens = (sparse_back + dot_cols(low_grad, left_one)).astype(jnp.bfloat16)
    loss_scale = lax.rsqrt(jnp.float32(row_count * tok_count))
    terms = (
        loss_scale
        * jnp.einsum(
            "nseb,neqf->eqsbf", gathered, grad_pre_r, preferred_element_type=jnp.float32
        ).reshape(w_first.shape),
        loss_scale
        * jnp.einsum(
            "neqf,nseo->eqsfo", hidden_r, grad_in, preferred_element_type=jnp.float32
        ).reshape(w_second.shape),
        loss_scale * dot_rows(tokens, low_grad),
        loss_scale * dot_rows(low_in, grad_pre),
        loss_scale * dot_rows(hidden, low_back),
        loss_scale * dot_rows(low_mid, cotangent),
    )
    shares = (
        lax.psum_scatter(
            terms[0].astype(jnp.bfloat16), "tok", scatter_dimension=2, tiled=True
        ).astype(jnp.float32),
        lax.psum_scatter(
            terms[1].astype(jnp.bfloat16), "tok", scatter_dimension=2, tiled=True
        ).astype(jnp.float32),
        lax.psum_scatter(
            terms[2].astype(jnp.bfloat16), "tok", scatter_dimension=0, tiled=True
        ).astype(jnp.float32),
        lax.psum_scatter(
            terms[3].astype(jnp.bfloat16), "tok", scatter_dimension=1, tiled=True
        ).astype(jnp.float32),
        lax.psum_scatter(
            terms[4].astype(jnp.bfloat16), "tok", scatter_dimension=0, tiled=True
        ).astype(jnp.float32),
        lax.psum_scatter(
            terms[5].astype(jnp.bfloat16), "tok", scatter_dimension=1, tiled=True
        ).astype(jnp.float32),
    )
    return (
        layer_out,
        grad_tokens,
        shares[0].astype(jnp.bfloat16),
        shares[2].astype(jnp.bfloat16),
        shares[3].astype(jnp.bfloat16),
        shares[1].astype(jnp.bfloat16),
        shares[4].astype(jnp.bfloat16),
        shares[5].astype(jnp.bfloat16),
    )


def solution(mesh):
    return jax.shard_map(
        local,
        mesh=mesh,
        in_specs=(
            P("tok", "hid"),
            P("hid", None, "tok", None),
            P(("hid", "tok"), None),
            P(None, ("hid", "tok")),
            P(),
            P("hid", None, "tok", None),
            P(("hid", "tok"), None),
            P(None, ("hid", "tok")),
            P(),
            P("tok", "hid"),
        ),
        out_specs=(
            P("tok", "hid"),
            P("tok", "hid"),
            P("hid", None, "tok", None),
            P(("hid", "tok"), None),
            P(None, ("hid", "tok")),
            P("hid", None, "tok", None),
            P(("hid", "tok"), None),
            P(None, ("hid", "tok")),
        ),
        check_vma=False,
    )
```

profile of v0, /device:TPU:0, one launch (start us, length us, event | category | flops | bytes accessed | tf_op | source)
XLA Modules:
  0.0 1396.9 jit_solution(3682937672715421164)
XLA Ops:
  13.0 17.4 %all_gather.26 = bf16[1024,256]{1,0:T(8,128)(2,1)S(1)} all-gather(bf16[256,256]{1,0:T(8,128)(2,1)S(1)} %copy-done.12), channel_id=1, replica_groups=mesh['hid'=8,'tok'=4] {'tok'}, dimensions={0}, use_global_device_ids=true | all-gather | bytes 655360 | tf_op jit(solution)/shard_map/all_gather | solution.py:88
  31.5 16.3 %all_gather.30 = bf16[256,1024]{1,0:T(8,128)(2,1)S(1)} all-gather(bf16[256,256]{1,0:T(8,128)(2,1)S(1)} %copy-done.13), channel_id=1, replica_groups=mesh['hid'=8,'tok'=4] {'tok'}, dimensions={1}, use_global_device_ids=true | all-gather | bytes 655360 | tf_op jit(solution)/shard_map/all_gather | solution.py:91
  48.9 32.9 %all-reduce.4 = (bf16[224,256]{1,0:T(8,128)(2,1)S(1)}, bf16[224,256]{1,0:T(8,128)(2,1)S(1)}) all-reduce(f32[224,256]{1,0:T(8,128)S(1)} %fusion.60, f32[224,256]{1,0:T(8,128)S(1)} %fusion.62), channel_id=1, replica_groups=mesh['hid'=8,'tok'=4] {'hid'}, use_global_device_ids=true, to_apply=%region_0.0 | all-reduce | flops 114688 | bytes 688128 | tf_op jit(solution)/shard_map/psum | solution.py:35
  90.8 11.0 gather_fusion.1
  101.8 10.5 gather_fusion
  112.3 194.0 %all-gather.13.cloned.1.call-done = bf16[16,6,256,256]{3,2,1,0:T(8,128)(2,1)} async-done(((bf16[16,6,64,256]{3,2,1,0:T(8,128)(2,1)}), bf16[16,6,256,256]{3,2,1,0:T(8,128)(2,1)}) %all-gather.13.cloned.1.call-update) | async-done | bytes 12582928 | tf_op jit(solution)/shard_map/all_gather | solution.py:87
  306.3 10.4 fusion.57
  318.8 205.9 %all-gather.9.cloned.1.call-done = bf16[16,6,256,256]{3,2,0,1:T(8,128)(2,1)} async-done(((bf16[16,6,64,256]{3,2,0,1:T(8,128)(2,1)}), bf16[16,6,256,256]{3,2,0,1:T(8,128)(2,1)}) %all-gather.9.cloned.1.call-update) | async-done | bytes 12582928 | tf_op jit(solution)/shard_map/all_gather | solution.py:86
  524.7 12.0 fusion.56
  539.1 31.2 %all-gather.11.cloned.1.call-done = bf16[256,4096]{1,0:T(8,128)(2,1)} async-done(((bf16[256,1024]{1,0:T(8,128)(2,1)}), bf16[256,4096]{1,0:T(8,128)(2,1)}) %all-gather.11.cloned.1.call-update) | async-done | bytes 2097168 | tf_op jit(solution)/shard_map/all_gather | solution.py:89
  570.3 6.7 multiply_convert_fusion.2
  577.0 39.4 %all-gather.15.cloned.1.call-done = bf16[4096,256]{1,0:T(8,128)(2,1)} async-done(((bf16[1024,256]{1,0:T(8,128)(2,1)}), bf16[4096,256]{1,0:T(8,128)(2,1)}) %all-gather.15.cloned.1.call-update) | async-done | bytes 2097168 | tf_op jit(solution)/shard_map/all_gather | solution.py:90
  616.4 6.0 fusion.24
  625.2 29.4 %all-reduce.5 = (bf16[224,256]{1,0:T(8,128)(2,1)S(1)}, bf16[224,256]{1,0:T(8,128)(2,1)S(1)}) all-reduce(f32[224,256]{1,0:T(8,128)S(1)} %fusion.61, f32[224,256]{1,0:T(8,128)S(1)} %fusion.63), channel_id=1, replica_groups=mesh['hid'=8,'tok'=4] {'hid'}, use_global_device_ids=true, to_apply=%region_2.0 | all-reduce | flops 114688 | bytes 688128 | tf_op jit(solution)/shard_map/psum | solution.py:35
  657.6 13.2 fusion.14
  670.8 28.7 %fusion = f32[32,224,256,1]{2,0,3,1:T(8,128)S(1)} fusion(f32[224,6,16,256]{3,0,1,2:T(8,128)} %fusion.14, s32[6,16]{1,0:T(8,128)S(1)} %get-tuple-element.47), kind=kOutput, calls=%fused_computation.4 | convolution fusion | flops 2113932288 | bytes 29360512 | tf_op jit(solution)/shard_map/nsho,shc->nco/dot_general | solution.py:54
  699.5 9.4 copy.94
  711.0 16.4 %convolution_bitcast_fusion = f32[224,6,16,256]{3,0,1,2:T(8,128)} fusion(bf16[16,6,256,256]{3,2,1,0:T(8,128)(2,1)} %all-gather.13.cloned.1.call-done, bf16[224,16,256,1]{2,1,0,3:T(8,128)(2,1)S(1)} %bitcast.141), kind=kOutput, calls=%fused_computation.19 | convolution fusion | flops 2818572288 | bytes 36438016 | tf_op jit(solution)/shard_map/neqf,eqsfo->nseo/dot_general | solution.py:116
  727.4 28.5 %fusion.2 = f32[32,224,256,1]{2,0,3,1:T(8,128)S(1)} fusion(f32[224,6,16,256]{3,0,1,2:T(8,128)} %convolution_bitcast_fusion, s32[6,16]{1,0:T(8,128)S(1)} %get-tuple-element.45), kind=kOutput, calls=%fused_computation.6 | convolution fusion | flops 2113932288 | bytes 29360512 | tf_op jit(solution)/shard_map/nsho,shc->nco/dot_general | solution.py:54
  755.9 9.5 copy.91
  765.5 11.5 fusion.5
  777.0 17.2 %copy.69 = bf16[16,6,256,256]{3,0,1,2:T(8,128)(2,1)} copy(bf16[16,6,256,256]{2,3,1,0:T(8,128)(2,1)} %fusion.5) | data formatting | bytes 25165824 | tf_op jit(solution)/shard_map/convert_element_type | solution.py:156
  794.2 12.0 fusion.4
  806.3 17.0 %copy.66 = bf16[16,6,256,256]{3,0,1,2:T(8,128)(2,1)} copy(bf16[16,6,256,256]{2,3,1,0:T(8,128)(2,1)} %fusion.4) | data formatting | bytes 25165824 | tf_op jit(solution)/shard_map/convert_element_type | solution.py:153
  835.2 8.8 reduce-scatter.9.cloned.1.call-done
  846.3 211.8 %reduce-scatter.19.cloned.1.call-done = bf16[16,6,64,256]{3,0,1,2:T(8,128)(2,1)} async-done(((bf16[16,6,256,256]{3,0,1,2:T(8,128)(2,1)}), bf16[16,6,64,256]{3,0,1,2:T(8,128)(2,1)}) %reduce-scatter.19.cloned.1.call-update) | async-done | bytes 3145744 | tf_op jit(solution)/shard_map/reduce_scatter | solution.py:155
  1058.2 5.3 copy.72
  1063.5 209.9 %reduce-scatter.13.cloned.1.call-done = bf16[16,6,64,256]{3,0,1,2:T(8,128)(2,1)} async-done(((bf16[16,6,256,256]{3,0,1,2:T(8,128)(2,1)}), bf16[16,6,64,256]{3,0,1,2:T(8,128)(2,1)}) %reduce-scatter.13.cloned.1.call-update) | async-done | bytes 3145744 | tf_op jit(solution)/shard_map/reduce_scatter | solution.py:152
  1273.4 5.3 copy.70
  1278.8 20.1 %reduce-scatter.23.cloned.1.call-done = bf16[256,256]{1,0:T(8,128)(2,1)} async-done(((bf16[256,1024]{1,0:T(8,128)(2,1)}), bf16[256,256]{1,0:T(8,128)(2,1)}) %reduce-scatter.23.cloned.1.call-update) | async-done | bytes 131088 | tf_op jit(solution)/shard_map/reduce_scatter | solution.py:167
  1298.9 45.0 %reduce-scatter.21.cloned.1.call-done = bf16[1024,256]{1,0:T(8,128)(2,1)} async-done(((bf16[4096,256]{1,0:T(8,128)(2,1)}), bf16[1024,256]{1,0:T(8,128)(2,1)}) %reduce-scatter.21.cloned.1.call-update) | async-done | bytes 524304 | tf_op jit(solution)/shard_map/reduce_scatter | solution.py:164
  1343.9 46.0 %reduce-scatter.17.cloned.1.call-done = bf16[256,1024]{1,0:T(8,128)(2,1)} async-done(((bf16[256,4096]{1,0:T(8,128)(2,1)}), bf16[256,1024]{1,0:T(8,128)(2,1)}) %reduce-scatter.17.cloned.1.call-update) | async-done | bytes 524304 | tf_op jit(solution)/shard_map/reduce_scatter | solution.py:161
  (88 shorter events, 43.5 us)
Async XLA Ops:
  7.2 2.3 copy-start.10
  7.2 74.7 %all-gather.7.cloned.1.call-start = ((), (), s32[]{:S(2)}) async-start(), calls=%async_computation.8 | async-start | bytes 4128768 | tf_op jit(solution)/shard_map/all_gather | solution.py:43
  7.9 78.6 %all-gather.17.cloned.1.call-start = ((), (), s32[]{:S(2)}) async-start(), calls=%async_computation.14 | async-start | bytes 4128768 | tf_op jit(solution)/shard_map/all_gather | solution.py:43
  8.7 297.6 %all-gather.13.cloned.1.call-start = ((), (), s32[]{:S(2)}) async-start(), calls=%async_computation.11 | async-start | bytes 15728640 | tf_op jit(solution)/shard_map/all_gather | solution.py:87
  9.4 515.3 %all-gather.9.cloned.1.call-start = ((), (), s32[]{:S(2)}) async-start(), calls=%async_computation.9 | async-start | bytes 15728640 | tf_op jit(solution)/shard_map/all_gather | solution.py:86
  11.3 1.3 copy-start.14
  11.3 1.5 copy-start.15
  11.3 1.6 copy-start.12
  11.3 19.8 %copy-start.7 = (bf16[224,1024]{1,0:T(8,128)(2,1)S(1)}, bf16[224,1024]{1,0:T(8,128)(2,1)}, u32[]{:S(2)}) copy-start(bf16[224,1024]{1,0:T(8,128)(2,1)} %param.10) | copy-start | bytes 1376260
  11.3 20.1 %copy-start.13 = (bf16[256,256]{1,0:T(8,128)(2,1)S(1)}, bf16[256,256]{1,0:T(8,128)(2,1)}, u32[]{:S(2)}) copy-start(bf16[256,256]{1,0:T(8,128)(2,1)} %param.17) | copy-start | bytes 393220
  11.4 37.2 %copy-start.8 = (bf16[224,1024]{1,0:T(8,128)(2,1)S(1)}, bf16[224,1024]{1,0:T(8,128)(2,1)}, u32[]{:S(2)}) copy-start(bf16[224,1024]{1,0:T(8,128)(2,1)} %param.19) | copy-start | bytes 1376260
  11.4 558.9 %all-gather.11.cloned.1.call-start = ((), (), s32[]{:S(2)}) async-start(), calls=%async_computation.10 | async-start | bytes 2621440 | tf_op jit(solution)/shard_map/all_gather | solution.py:89
  12.0 604.4 %all-gather.15.cloned.1.call-start = ((), (), s32[]{:S(2)}) async-start(), calls=%async_computation.13 | async-start | bytes 2621440 | tf_op jit(solution)/shard_map/all_gather | solution.py:90
  12.6 818.7 %reduce-scatter.15.cloned.1.call-start = ((), (), s32[]{:S(2)}) async-start(), calls=%async_computation.17 | async-start | bytes 655360 | tf_op jit(solution)/shard_map/reduce_scatter | solution.py:158
  30.3 0.8 copy-start.5
  47.7 0.8 copy-start.3
  616.4 6.0 copy-start.2
  622.4 1.5 copy-start
  622.4 2.1 copy-start.11
  655.8 177.1 %reduce-scatter.11.cloned.1.call-start = ((), (), s32[]{:S(2)}) async-start(), calls=%async_computation.15 | async-start | bytes 8257536 | tf_op jit(solution)/shard_map/reduce_scatter | solution.py:55
  709.0 135.1 %reduce-scatter.9.cloned.1.call-start = ((), (), s32[]{:S(2)}) async-start(), calls=%async_computation.12 | async-start | bytes 8257536 | tf_op jit(solution)/shard_map/reduce_scatter | solution.py:55
  711.0 16.4 %copy-start.1 = (bf16[28,8,16,256]{3,2,1,0:T(8,128)(2,1)}, bf16[28,8,16,256]{3,2,1,0:T(8,128)(2,1)S(1)}, u32[]{:S(2)}) copy-start(bf16[28,8,16,256]{3,2,1,0:T(8,128)(2,1)S(1)} %copy.90) | copy-start | bytes 5505028
  765.5 292.7 %reduce-scatter.19.cloned.1.call-start = ((), (), s32[]{:S(2)}) async-start(), calls=%async_computation.19 | async-start | bytes 15728640 | tf_op jit(solution)/shard_map/reduce_scatter | solution.py:155
  794.2 479.3 %reduce-scatter.13.cloned.1.call-start = ((), (), s32[]{:S(2)}) async-start(), calls=%async_computation.16 | async-start | bytes 15728640 | tf_op jit(solution)/shard_map/reduce_scatter | solution.py:152
  823.3 1.0 copy-start.9
  823.3 475.6 %reduce-scatter.23.cloned.1.call-start = ((), (), s32[]{:S(2)}) async-start(), calls=%async_computation.21 | async-start | bytes 655360 | tf_op jit(solution)/shard_map/reduce_scatter | solution.py:167
  825.4 518.5 %reduce-scatter.21.cloned.1.call-start = ((), (), s32[]{:S(2)}) async-start(), calls=%async_computation.20 | async-start | bytes 2621440 | tf_op jit(solution)/shard_map/reduce_scatter | solution.py:164
  829.1 3.8 copy-start.6
  829.1 15.0 %copy-start.4 = (bf16[256,1024]{1,0:T(8,128)(2,1)S(1)}, bf16[256,1024]{1,0:T(8,128)(2,1)}, u32[]{:S(2)}) copy-start(bf16[256,1024]{1,0:T(8,128)(2,1)} %copy-done.3) | copy-start | bytes 1572868
  829.1 560.8 %reduce-scatter.17.cloned.1.call-start = ((), (), s32[]{:S(2)}) async-start(), calls=%async_computation.18 | async-start | bytes 2621440 | tf_op jit(solution)/shard_map/reduce_scatter | solution.py:161
Sparse Core Ops, SparseCore 0:
  9.9 37.2 all-gather.6
  49.1 37.3 all-gather.16
  88.0 218.1 all-gather.12
  308.3 216.3 all-gather.8
  526.1 44.1 all-gather.10
  571.7 44.6 all-gather.14
  656.0 19.1 reduce-scatter.14
  709.1 64.2 reduce-scatter.10
  777.1 66.9 reduce-scatter.8
  846.3 211.8 reduce-scatter.18
  1060.5 212.8 reduce-scatter.12
  1276.1 22.6 reduce-scatter.22
  1301.7 42.1 reduce-scatter.20
  1346.7 43.1 reduce-scatter.16
where the time goes:
time: 1410 us; the launch traced here: 1400 us
  waiting for transfers between devices  1020 us (72%)
  matrix products  160 us (11%)
  local copies, waits for them, and re-layouts  110 us (8%)
  blocking collectives  96 us (7%)
  between operations  14.6 us (1%)
    reduce_scatter x1, waiting for transfers between devices, local(): lax.psum_scatter(terms[1].astype(jnp.bfloat16), 'tok', scatter_dimension=...  212 us
    reduce_scatter x1, waiting for transfers between devices, local(): lax.psum_scatter(terms[0].astype(jnp.bfloat16), 'tok', scatter_dimension=...  210 us
    all_gather x1, waiting for transfers between devices, local(): lax.all_gather(in_blocks, 'tok', axis=2, tiled=True)  206 us
    all_gather x1, waiting for transfers between devices, local(): lax.all_gather(out_blocks, 'tok', axis=2, tiled=True)  194 us
    psum x2, blocking collectives, rank_sum(): return lax.psum(values, 'hid')  62.3 us
    dot_general x2, matrix products, scatter_out(): jnp.einsum('nsho,shc->nco', parts, picker, precision=lax.Precision.HIGHEST)  57.2 us
    reduce_scatter x1, waiting for transfers between devices, local(): lax.psum_scatter(terms[3].astype(jnp.bfloat16), 'tok', scatter_dimension=...  46 us
    unnamed x42, local copies, waits for them, and re-layouts  45.3 us
  transfers between devices with their start and end apart: 14, of which 11 were waited for; matrix products, arithmetic and copies ran while one was open for 18% of the time, Pallas kernels for 0%

commit v1 on v0

--- a/solution.py
+++ b/solution.py
@@ -5,6 +5,24 @@
 
 D = 8192
 BLK = 256
+
+
+def gather_around(array, axis, dim):
+    ways, here, step = (lax.axis_size(axis), lax.axis_index(axis), array.shape[dim])
+    shape = [n * ways if d == dim else n for d, n in enumerate(array.shape)]
+    full = lax.dynamic_update_slice_in_dim(
+        jnp.zeros(shape, array.dtype), array, here * step, axis=dim
+    )
+    going_up = going_down = array
+    for far in range(1, ways // 2 + 1):
+        going_up = lax.ppermute(going_up, axis, [(d, (d + 1) % ways) for d in range(ways)])
+        full = lax.dynamic_update_slice_in_dim(full, going_up, (here - far) % ways * step, axis=dim)
+        if 2 * far < ways:
+            going_down = lax.ppermute(going_down, axis, [(d, (d - 1) % ways) for d in range(ways)])
+            full = lax.dynamic_update_slice_in_dim(
+                full, going_down, (here + far) % ways * step, axis=dim
+            )
+    return full
 
 
 def gelu_parts(preact):
@@ -83,7 +101,7 @@
     blk_width = in_blocks.shape[3]
     tok_count = lax.axis_size("tok")
     w_first, w_second, left_one, right_one, left_two, right_two = (
-        lax.all_gather(in_blocks, "tok", axis=2, tiled=True),
+        gather_around(in_blocks, "tok", 2),
         lax.all_gather(out_blocks, "tok", axis=2, tiled=True),
         lax.all_gather(in_left, "tok", axis=0, tiled=True),
         lax.all_gather(in_right, "tok", axis=1, tiled=True),

time: 1410 us -> 1310 us (0.929)
  waiting for transfers between devices: 1020 us -> 701 us
  blocking collectives: 96 us -> 263 us
  starting transfers between devices: 0.56 us -> 30.7 us
  local copies, waits for them, and re-layouts: 110 us -> 126 us
    all_gather x1 -> x0, waiting for transfers between devices: 206 us -> none  [local(): lax.all_gather(in_blocks, 'tok', axis=2, tiled=True)]
    all_gather x1, blocking collectives: 17.4 us -> 177 us  [local(): lax.all_gather(in_left, 'tok', axis=0, tiled=True)]
    all_gather x1, waiting for transfers between devices: 194 us -> 60.4 us  [local(): lax.all_gather(out_blocks, 'tok', axis=2, tiled=True)]
    ppermute x0 -> x3, waiting for transfers between devices: none -> 93 us  [the longest x2 93 us: gather_around(): lax.ppermute(going_up, axis, [(d, (d + 1) % ways) for d in range(ways)])]
    all_gather x1, waiting for transfers between devices: 39.4 us -> 0.01 us  [local(): lax.all_gather(out_left, 'tok', axis=0, tiled=True)]
    all_gather x1, waiting for transfers between devices: 31.2 us -> 0.01 us  [local(): lax.all_gather(in_right, 'tok', axis=1, tiled=True)]
    ppermute x0 -> x3, starting transfers between devices: none -> 30.2 us  [the longest x2 28.1 us: gather_around(): lax.ppermute(going_up, axis, [(d, (d + 1) % ways) for d in range(ways)])]
    unnamed x42 -> x41, local copies, waits for them, and re-layouts: 45.3 us -> 43.4 us
  transfers between devices with their start and end apart: 14 -> 16, of which waited for: 11 -> 8; matrix products, arithmetic and copies ran while one was open for 18% -> 21% of each run, Pallas kernels for 0% -> 0%
where the time goes in v1:
time: 1310 us; the launch traced here: 1300 us
  waiting for transfers between devices  701 us (54%)
  blocking collectives  263 us (20%)
  matrix products  161 us (12%)
  local copies, waits for them, and re-layouts  126 us (10%)
  starting transfers between devices  30.7 us (2%)
  between operations  14.6 us (1%)
    reduce_scatter x1, waiting for transfers between devices, local(): lax.psum_scatter(terms[1].astype(jnp.bfloat16), 'tok', scatter_dimension=...  212 us
    reduce_scatter x1, waiting for transfers between devices, local(): lax.psum_scatter(terms[0].astype(jnp.bfloat16), 'tok', scatter_dimension=...  210 us
    all_gather x1, blocking collectives, local(): lax.all_gather(in_left, 'tok', axis=0, tiled=True)  177 us
    ppermute x2, waiting for transfers between devices, gather_around(): lax.ppermute(going_up, axis, [(d, (d + 1) % ways) for d in range(ways)])  93 us
    all_gather x1, waiting for transfers between devices, local(): lax.all_gather(out_blocks, 'tok', axis=2, tiled=True)  60.4 us
    psum x2, blocking collectives, rank_sum(): return lax.psum(values, 'hid')  59.5 us
    dot_general x2, matrix products, scatter_out(): jnp.einsum('nsho,shc->nco', parts, picker, precision=lax.Precision.HIGHEST)  57.6 us
    reduce_scatter x1, waiting for transfers between devices, local(): lax.psum_scatter(terms[3].astype(jnp.bfloat16), 'tok', scatter_dimension=...  45.1 us
  transfers between devices with their start and end apart: 16, of which 8 were waited for; matrix products, arithmetic and copies ran while one was open for 21% of the time, Pallas kernels for 0%

profile of v1, /device:TPU:0, one launch (start us, length us, event | category | flops | bytes accessed | tf_op | source)
XLA Modules:
  0.0 1296.4 jit_solution(5500704883681599650)
XLA Ops:
  15.8 93.0 %collective-permute-done = bf16[16,6,64,256]{3,2,1,0:T(8,128)(2,1)} collective-permute-done((bf16[16,6,64,256]{3,2,1,0:T(8,128)(2,1)}, bf16[16,6,64,256]{3,2,1,0:T(8,128)(2,1)}, u32[]{:S(2)}, u32[]{:S(2)}) %collective-permute-start) | collective-permute-done | bytes 3145760 | tf_op jit(solution)/shard_map/ppermute | solution.py:18
  108.8 25.0 %collective-permute-start.2 = (bf16[16,6,64,256]{3,2,1,0:T(8,128)(2,1)}, bf16[16,6,64,256]{3,2,1,0:T(8,128)(2,1)}, u32[]{:S(2)}, u32[]{:S(2)}) collective-permute-start(bf16[16,6,64,256]{3,2,1,0:T(8,128)(2,1)} %collective-permute-done), channel_id=1, source_target_pairs={{0,1},{1,2},{2,3},{3,0},{4,5},{5,6},{6,7},{7,4},{8,9},{9,10},{10,1... | collective-permute-start | bytes 9437192 | tf_op jit(solution)/shard_map/ppermute | solution.py:18
  134.0 176.6 %all_gather.22 = bf16[1024,256]{1,0:T(8,128)(2,1)S(1)} all-gather(bf16[256,256]{1,0:T(8,128)(2,1)S(1)} %copy-done.12), channel_id=1, replica_groups=mesh['hid'=8,'tok'=4] {'tok'}, dimensions={0}, use_global_device_ids=true | all-gather | bytes 655360 | tf_op jit(solution)/shard_map/all_gather | solution.py:106
  311.7 27.1 %all_gather.26 = bf16[256,1024]{1,0:T(8,128)(2,1)S(1)} all-gather(bf16[256,256]{1,0:T(8,128)(2,1)S(1)} %copy-done.13), channel_id=1, replica_groups=mesh['hid'=8,'tok'=4] {'tok'}, dimensions={1}, use_global_device_ids=true | all-gather | bytes 655360 | tf_op jit(solution)/shard_map/all_gather | solution.py:109
  340.1 29.4 %all-reduce.4 = (bf16[224,256]{1,0:T(8,128)(2,1)S(1)}, bf16[224,256]{1,0:T(8,128)(2,1)S(1)}) all-reduce(f32[224,256]{1,0:T(8,128)S(1)} %fusion.62, f32[224,256]{1,0:T(8,128)S(1)} %fusion.64), channel_id=1, replica_groups=mesh['hid'=8,'tok'=4] {'hid'}, use_global_device_ids=true, to_apply=%region_0.1 | all-reduce | flops 114688 | bytes 688128 | tf_op jit(solution)/shard_map/psum | solution.py:53
  369.6 6.1 broadcast.44
  389.4 4.4 copy.131
  393.8 10.1 gather_fusion
  403.9 12.8 fusion.59
  421.0 6.1 multiply_convert_fusion.2
  435.5 10.2 gather_fusion.1
  445.7 60.4 %all-gather.10.cloned.1.call-done = bf16[16,6,256,256]{3,2,1,0:T(8,128)(2,1)} async-done(((bf16[16,6,64,256]{3,2,1,0:T(8,128)(2,1)}), bf16[16,6,256,256]{3,2,1,0:T(8,128)(2,1)}) %all-gather.10.cloned.1.call-update) | async-done | bytes 12582928 | tf_op jit(solution)/shard_map/all_gather | solution.py:105
  506.1 10.0 fusion.56
  522.6 30.0 %all-reduce.5 = (bf16[224,256]{1,0:T(8,128)(2,1)S(1)}, bf16[224,256]{1,0:T(8,128)(2,1)S(1)}) all-reduce(f32[224,256]{1,0:T(8,128)S(1)} %fusion.63, f32[224,256]{1,0:T(8,128)S(1)} %fusion.65), channel_id=1, replica_groups=mesh['hid'=8,'tok'=4] {'hid'}, use_global_device_ids=true, to_apply=%region_2.3 | all-reduce | flops 114688 | bytes 688128 | tf_op jit(solution)/shard_map/psum | solution.py:53
  553.9 16.0 %convolution_bitcast_fusion.1 = f32[224,6,16,256]{3,0,1,2:T(8,128)} fusion(bf16[16,6,256,256]{3,2,1,0:T(8,128)(2,1)} %all-gather.10.cloned.1.call-done, bf16[224,16,256,1]{2,1,0,3:T(8,128)(2,1)} %bitcast.139), kind=kOutput, calls=%fused_computation.19 | convolution fusion | flops 2818572288 | bytes 36438016 | tf_op jit(solution)/shard_map/neqf,eqsfo->nseo/dot_general | solution.py:134
  569.9 29.1 %fusion.2 = f32[32,224,256,1]{2,0,3,1:T(8,128)S(1)} fusion(f32[224,6,16,256]{3,0,1,2:T(8,128)} %convolution_bitcast_fusion.1, s32[6,16]{1,0:T(8,128)S(1)} %get-tuple-element.45), kind=kOutput, calls=%fused_computation.6 | convolution fusion | flops 2113932288 | bytes 29360512 | tf_op jit(solution)/shard_map/nsho,shc->nco/dot_general | solution.py:72
  598.9 9.5 copy.90
  610.2 15.1 %convolution_bitcast_fusion = f32[224,6,16,256]{3,0,1,2:T(8,128)} fusion(bf16[16,6,256,256]{3,2,1,0:T(8,128)(2,1)} %constant_dynamic-update-slice_fusion, bf16[224,16,256,1]{2,1,0,3:T(8,128)(2,1)} %bitcast.137), kind=kOutput, calls=%fused_computation.18 | convolution fusion | flops 2818572288 | bytes 36438016 | tf_op jit(solution)/shard_map/neqf,eqsbf->nseb/dot_general | solution.py:149
  625.3 28.5 %fusion = f32[32,224,256,1]{2,0,3,1:T(8,128)S(1)} fusion(f32[224,6,16,256]{3,0,1,2:T(8,128)} %convolution_bitcast_fusion, s32[6,16]{1,0:T(8,128)S(1)} %get-tuple-element.47), kind=kOutput, calls=%fused_computation.4 | convolution fusion | flops 2113932288 | bytes 29360512 | tf_op jit(solution)/shard_map/nsho,shc->nco/dot_general | solution.py:72
  653.8 9.4 copy.93
  663.3 11.5 fusion.5
  674.8 17.3 %copy.67 = bf16[16,6,256,256]{3,0,1,2:T(8,128)(2,1)} copy(bf16[16,6,256,256]{2,3,1,0:T(8,128)(2,1)} %fusion.5) | data formatting | bytes 25165824 | tf_op jit(solution)/shard_map/convert_element_type | solution.py:174
  692.2 12.2 fusion.4
  704.4 16.4 %copy.64 = bf16[16,6,256,256]{3,0,1,2:T(8,128)(2,1)} copy(bf16[16,6,256,256]{2,3,1,0:T(8,128)(2,1)} %fusion.4) | data formatting | bytes 25165824 | tf_op jit(solution)/shard_map/convert_element_type | solution.py:171
  732.2 11.3 reduce-scatter.11.cloned.1.call-done
  745.7 212.0 %reduce-scatter.19.cloned.1.call-done = bf16[16,6,64,256]{3,0,1,2:T(8,128)(2,1)} async-done(((bf16[16,6,256,256]{3,0,1,2:T(8,128)(2,1)}), bf16[16,6,64,256]{3,0,1,2:T(8,128)(2,1)}) %reduce-scatter.19.cloned.1.call-update) | async-done | bytes 3145744 | tf_op jit(solution)/shard_map/reduce_scatter | solution.py:173
  957.7 5.3 copy.70
  963.0 209.8 %reduce-scatter.13.cloned.1.call-done = bf16[16,6,64,256]{3,0,1,2:T(8,128)(2,1)} async-done(((bf16[16,6,256,256]{3,0,1,2:T(8,128)(2,1)}), bf16[16,6,64,256]{3,0,1,2:T(8,128)(2,1)}) %reduce-scatter.13.cloned.1.call-update) | async-done | bytes 3145744 | tf_op jit(solution)/shard_map/reduce_scatter | solution.py:170
  1172.8 5.3 copy.68
  1178.1 42.5 %reduce-scatter.21.cloned.1.call-done = bf16[1024,256]{1,0:T(8,128)(2,1)} async-done(((bf16[4096,256]{1,0:T(8,128)(2,1)}), bf16[1024,256]{1,0:T(8,128)(2,1)}) %reduce-scatter.21.cloned.1.call-update) | async-done | bytes 524304 | tf_op jit(solution)/shard_map/reduce_scatter | solution.py:182
  1220.6 23.8 %reduce-scatter.23.cloned.1.call-done = bf16[256,256]{1,0:T(8,128)(2,1)} async-done(((bf16[256,1024]{1,0:T(8,128)(2,1)}), bf16[256,256]{1,0:T(8,128)(2,1)}) %reduce-scatter.23.cloned.1.call-update) | async-done | bytes 131088 | tf_op jit(solution)/shard_map/reduce_scatter | solution.py:185
  1244.4 45.1 %reduce-scatter.17.cloned.1.call-done = bf16[256,1024]{1,0:T(8,128)(2,1)} async-done(((bf16[256,4096]{1,0:T(8,128)(2,1)}), bf16[256,1024]{1,0:T(8,128)(2,1)}) %reduce-scatter.17.cloned.1.call-update) | async-done | bytes 524304 | tf_op jit(solution)/shard_map/reduce_scatter | solution.py:179
  (95 shorter events, 60.6 us)
Async XLA Ops:
  7.2 304.2 %copy-start.6 = (bf16[224,1024]{1,0:T(8,128)(2,1)S(1)}, bf16[224,1024]{1,0:T(8,128)(2,1)}, u32[]{:S(2)}) copy-start(bf16[224,1024]{1,0:T(8,128)(2,1)} %param.10) | copy-start | bytes 1376260
  7.2 126.7 %copy-start.14 = (s32[128,6]{0,1:T(8,128)S(1)}, s32[128,6]{0,1:T(8,128)}, u32[]{:S(2)}) copy-start(s32[128,6]{0,1:T(8,128)} %param.14) | copy-start | bytes 9220
  7.2 126.8 %copy-start.12 = (bf16[256,256]{1,0:T(8,128)(2,1)S(1)}, bf16[256,256]{1,0:T(8,128)(2,1)}, u32[]{:S(2)}) copy-start(bf16[256,256]{1,0:T(8,128)(2,1)} %param.12) | copy-start | bytes 393220
  7.2 304.5 %copy-start.13 = (bf16[256,256]{1,0:T(8,128)(2,1)S(1)}, bf16[256,256]{1,0:T(8,128)(2,1)}, u32[]{:S(2)}) copy-start(bf16[256,256]{1,0:T(8,128)(2,1)} %param.17) | copy-start | bytes 393220
  7.2 382.2 %all-gather.6.cloned.1.call-start = ((), (), s32[]{:S(2)}) async-start(), calls=%async_computation.8 | async-start | bytes 4128768 | tf_op jit(solution)/shard_map/all_gather | solution.py:61
  7.9 331.6 %copy-start.7 = (bf16[224,1024]{1,0:T(8,128)(2,1)S(1)}, bf16[224,1024]{1,0:T(8,128)(2,1)}, u32[]{:S(2)}) copy-start(bf16[224,1024]{1,0:T(8,128)(2,1)} %param.19) | copy-start | bytes 1376260
  8.0 413.0 %all-gather.8.cloned.1.call-start = ((), (), s32[]{:S(2)}) async-start(), calls=%async_computation.9 | async-start | bytes 2621440 | tf_op jit(solution)/shard_map/all_gather | solution.py:107
  8.7 420.2 %all-gather.12.cloned.1.call-start = ((), (), s32[]{:S(2)}) async-start(), calls=%async_computation.12 | async-start | bytes 2621440 | tf_op jit(solution)/shard_map/all_gather | solution.py:108
  9.4 330.5 %copy-start.15 = (s32[128,6]{0,1:T(8,128)S(1)}, s32[128,6]{0,1:T(8,128)}, u32[]{:S(2)}) copy-start(s32[128,6]{0,1:T(8,128)} %param.18) | copy-start | bytes 9220
  9.4 421.7 %all-gather.14.cloned.1.call-start = ((), (), s32[]{:S(2)}) async-start(), calls=%async_computation.13 | async-start | bytes 4128768 | tf_op jit(solution)/shard_map/all_gather | solution.py:61
  10.0 496.1 %all-gather.10.cloned.1.call-start = ((), (), s32[]{:S(2)}) async-start(), calls=%async_computation.10 | async-start | bytes 15728640 | tf_op jit(solution)/shard_map/all_gather | solution.py:105
  10.6 717.5 %reduce-scatter.15.cloned.1.call-start = ((), (), s32[]{:S(2)}) async-start(), calls=%async_computation.16 | async-start | bytes 655360 | tf_op jit(solution)/shard_map/reduce_scatter | solution.py:176
  10.7 98.2 %collective-permute-start = (bf16[16,6,64,256]{3,2,1,0:T(8,128)(2,1)}, bf16[16,6,64,256]{3,2,1,0:T(8,128)(2,1)}, u32[]{:S(2)}, u32[]{:S(2)}) collective-permute-start(bf16[16,6,64,256]{3,2,1,0:T(8,128)(2,1)} %param.11), channel_id=1, source_target_pairs={{0,1},{1,2},{2,3},{3,0},{4,5},{5,6},{6,7},{7,4},{8,9},{9,10},{10,1... | collective-permute-start | bytes 9437192 | tf_op jit(solution)/shard_map/ppermute | solution.py:18
  13.7 367.8 %collective-permute-start.1 = (bf16[16,6,64,256]{3,2,1,0:T(8,128)(2,1)}, bf16[16,6,64,256]{3,2,1,0:T(8,128)(2,1)}, u32[]{:S(2)}, u32[]{:S(2)}) collective-permute-start(bf16[16,6,64,256]{3,2,1,0:T(8,128)(2,1)} %param.11), channel_id=1, source_target_pairs={{0,3},{1,0},{2,1},{3,2},{4,7},{5,4},{6,5},{7,6},{8,11},{9,8},{10,9... | collective-permute-start | bytes 9437192 | tf_op jit(solution)/shard_map/ppermute | solution.py:21
  108.8 276.7 %collective-permute-start.2 = (bf16[16,6,64,256]{3,2,1,0:T(8,128)(2,1)}, bf16[16,6,64,256]{3,2,1,0:T(8,128)(2,1)}, u32[]{:S(2)}, u32[]{:S(2)}) collective-permute-start(bf16[16,6,64,256]{3,2,1,0:T(8,128)(2,1)} %collective-permute-done), channel_id=1, source_target_pairs={{0,1},{1,2},{2,3},{3,0},{4,5},{5,6},{6,7},{7,4},{8,9},{9,10},{10,1... | collective-permute-start | bytes 9437192 | tf_op jit(solution)/shard_map/ppermute | solution.py:18
  310.6 0.8 copy-start.2
  338.8 0.8 copy-start.4
  369.5 6.2 copy-start.10
  427.0 4.1 copy-start
  516.1 2.0 copy-start.9
  516.2 2.7 copy-start.11
  518.9 2.9 copy-start.1
  553.8 176.0 %reduce-scatter.9.cloned.1.call-start = ((), (), s32[]{:S(2)}) async-start(), calls=%async_computation.11 | async-start | bytes 8257536 | tf_op jit(solution)/shard_map/reduce_scatter | solution.py:73
  608.4 135.1 %reduce-scatter.11.cloned.1.call-start = ((), (), s32[]{:S(2)}) async-start(), calls=%async_computation.14 | async-start | bytes 8257536 | tf_op jit(solution)/shard_map/reduce_scatter | solution.py:73
  663.3 294.4 %reduce-scatter.19.cloned.1.call-start = ((), (), s32[]{:S(2)}) async-start(), calls=%async_computation.18 | async-start | bytes 15728640 | tf_op jit(solution)/shard_map/reduce_scatter | solution.py:173
  692.2 480.6 %reduce-scatter.13.cloned.1.call-start = ((), (), s32[]{:S(2)}) async-start(), calls=%async_computation.15 | async-start | bytes 15728640 | tf_op jit(solution)/shard_map/reduce_scatter | solution.py:170
  720.9 3.8 copy-start.8
  720.9 499.8 %reduce-scatter.21.cloned.1.call-start = ((), (), s32[]{:S(2)}) async-start(), calls=%async_computation.19 | async-start | bytes 2621440 | tf_op jit(solution)/shard_map/reduce_scatter | solution.py:182
  724.6 519.8 %reduce-scatter.23.cloned.1.call-start = ((), (), s32[]{:S(2)}) async-start(), calls=%async_computation.20 | async-start | bytes 655360 | tf_op jit(solution)/shard_map/reduce_scatter | solution.py:185
  725.8 3.9 copy-start.5
  725.9 17.6 %copy-start.3 = (bf16[1024,256]{1,0:T(8,128)(2,1)S(1)}, bf16[1024,256]{1,0:T(8,128)(2,1)}, u32[]{:S(2)}) copy-start(bf16[1024,256]{1,0:T(8,128)(2,1)} %copy-done.2) | copy-start | bytes 1572868
  725.9 563.6 %reduce-scatter.17.cloned.1.call-start = ((), (), s32[]{:S(2)}) async-start(), calls=%async_computation.17 | async-start | bytes 2621440 | tf_op jit(solution)/shard_map/reduce_scatter | solution.py:179
Sparse Core Ops, SparseCore 0:
  9.9 37.2 all-gather.5
  48.8 86.3 all-gather.7
  136.8 74.0 all-gather.11
  212.6 58.6 all-gather.13
  272.7 233.3 all-gather.9
  553.9 19.0 reduce-scatter.14
  608.5 64.1 reduce-scatter.8
  676.5 66.9 reduce-scatter.10
  745.8 211.8 reduce-scatter.18
  959.9 212.8 reduce-scatter.12
  1175.7 44.9 reduce-scatter.20
  1223.5 20.9 reduce-scatter.22
  1247.4 42.0 reduce-scatter.16
